TPU v7x, 32 devices: a whole 2x2x4 slice. The times are simulated.
32 devices in a mesh: row: 8 (over y, x, core), col: 4 (over z).
Axes of the slice: x: 2, y: 2, z: 4, core: 2. Of those that a mesh axis runs over, the one named last changes fastest.
Arguments:
- matrix: float32 [8, 3, 256, 4, 6, 256], P('row', None, None, 'col'), as said below
- checksum: float32 [8, 3, 256, 6, 256], P('row'), as said below
- failed: int32 [4], P('col'), may hold values from 0 to 3, as said below
Outputs:
- factored: float32 [8, 3, 256, 4, 6, 256], P('row', None, None, 'col')
- updated_checksum_result: float32 [8, 3, 256, 6, 256], P('row')
Inputs may be any that keep to these rules, and one draw needn't show every extreme that they name: `failed`: a permutation of the grid column indices; entry 0 names the grid column whose tiles in matrix carry no information. With the lost grid column rebuilt from checksum, matrix is symmetric positive definite. `checksum`: for each grid row, the sum over all grid columns of the intact matrix's tiles, the lost column included.
All inputs are finite; a program needn't handle non-finite values.
Results may differ from a plain program's by a relative error of at most 0.0003.
Values sent between devices are 32-bit elements; how exact they have to be, the bound alone decides.
A program may use at most 128 MiB of HBM per device.

v0:
```python
import jax
import jax.numpy as jnp
from jax import lax
from jax.sharding import PartitionSpec as P

PANELS = 3
EXACT = lax.Precision.HIGHEST
FAST = lax.Precision.HIGH


def dot_t(a, b, precision=EXACT):
    return lax.dot_general(a, b, (((1,), (1,)), ((), ())), precision=precision)


def dot(a, b, precision=EXACT):
    return lax.dot_general(a, b, (((1,), (0,)), ((), ())), precision=precision)


def shards(matrix, checksum, failed):
    rows_count = lax.axis_size("row")
    cols_count = lax.axis_size("col")
    row_index = lax.axis_index("row")
    column_position = lax.axis_index("col")
    tile_rows, width, tile_cols = (matrix.shape[1], matrix.shape[2], matrix.shape[4])
    own = matrix.reshape(tile_rows, width, tile_cols, width).transpose(0, 2, 1, 3)
    totals = checksum.reshape(tile_rows, width, tile_cols, width).transpose(0, 2, 1, 3)
    row_tiles = row_index + jnp.arange(tile_rows, dtype=jnp.int32) * rows_count
    col_tiles = column_position + jnp.arange(tile_cols, dtype=jnp.int32) * cols_count
    slots = (PANELS - 1) // cols_count + 1
    top_slots = (PANELS - 1) // rows_count + 1
    lost_column = lax.all_gather(failed, "col", axis=0, tiled=True)[0]
    lost = column_position == lost_column
    gathered = lax.all_gather(own[:, :slots], "col", axis=0)
    ids = jnp.arange(cols_count, dtype=jnp.int32).reshape(-1, 1, 1, 1, 1)
    others = jnp.sum(jnp.where(ids != lost_column, gathered, 0.0), axis=0)
    patch = totals[:, :slots] - others
    panels = []
    for k in range(PANELS):
        slot = k // cols_count
        panels.append(
            jnp.where(
                lost_column == k % cols_count, patch[:, slot], gathered[k % cols_count, :, slot]
            )
        )
    lead = jnp.stack(
        [
            jnp.where(
                row_index == i % rows_count,
                jnp.stack(
                    [panels[k][i // rows_count] for k in range(i + 1)]
                    + [jnp.zeros((width, width), jnp.float32) for _ in range(i + 1, PANELS)]
                ),
                0.0,
            )
            for i in range(PANELS)
        ]
    )
    lead = lax.psum(lead, "row")
    need = [
        tile_cols if a < top_slots else min(tile_cols, (rows_count * (a + 1) - 1) // cols_count + 1)
        for a in range(tile_rows)
    ]
    packed = jnp.concatenate([own[a, : need[a]] for a in range(tile_rows)], axis=0)
    lead_done, packed = lax.optimization_barrier((lead, packed))
    lead = lead_done
    summed = lax.psum(jnp.where(lost, 0.0, packed), "col")
    filled = []
    start = 0
    for a in range(tile_rows):
        pad = jnp.zeros((tile_cols - need[a], width, width), jnp.float32)
        filled.append(jnp.concatenate([summed[start : start + need[a]], pad], axis=0))
        start += need[a]
    work = jnp.where(lost, totals - jnp.stack(filled), own)
    tops = jnp.stack(
        [
            jnp.where(
                row_index == i % rows_count,
                jnp.concatenate([work[i // rows_count], totals[i // rows_count]], axis=0),
                0.0,
            )
            for i in range(PANELS)
        ]
    )
    tops = lax.psum(tops, "row")
    identity = jnp.eye(width, dtype=jnp.float32)
    factor = {}
    inverse = []
    for k in range(PANELS):
        for i in range(k, PANELS):
            tile = lead[i, k]
            for m in range(k):
                tile = tile - dot_t(factor[i, m], factor[k, m])
            if i == k:
                factor[k, k] = jnp.linalg.cholesky(tile)
                inverse.append(
                    jax.scipy.linalg.solve_triangular(factor[k, k], identity, lower=True)
                )
            else:
                factor[i, k] = dot_t(tile, inverse[k])
    solved_rows = []
    for k in range(PANELS):
        block = panels[k].reshape(tile_rows * width, width)
        for m in range(k):
            block = block - dot_t(solved_rows[m], factor[k, m])
        block = dot_t(block, inverse[k]).reshape(tile_rows, width, width)
        block = jnp.where((row_tiles > k)[:, None, None], block, 0.0)
        block = jnp.where((row_tiles == k)[:, None, None], factor[k, k][None], block)
        solved_rows.append(block.reshape(tile_rows * width, width))
    flat = tops.transpose(0, 2, 1, 3).reshape(PANELS, width, 2 * tile_cols * width)
    solved_cols = []
    for k in range(PANELS):
        block = flat[k]
        for m in range(k):
            block = block - dot(factor[k, m], solved_cols[m])
        solved_cols.append(dot(inverse[k], block))
    rows_factor = jnp.concatenate(solved_rows, axis=1)
    cols_factor = jnp.concatenate(solved_cols, axis=0)
    split = tile_cols * width
    shape = (tile_rows, width, tile_cols, width)
    update = dot(rows_factor, cols_factor[:, :split], FAST).reshape(shape).transpose(0, 2, 1, 3)
    drop = dot(rows_factor, cols_factor[:, split:], FAST).reshape(shape).transpose(0, 2, 1, 3)
    new_totals = (totals - drop).transpose(0, 2, 1, 3)
    work = work - update
    front = []
    for b in range(slots):
        tiles = work[:, b]
        for k in range(PANELS):
            if k // cols_count == b:
                mine = solved_rows[k].reshape(tile_rows, width, width)
                tiles = jnp.where(column_position == k % cols_count, mine, tiles)
        front.append(tiles)
    work = jnp.concatenate([jnp.stack(front, axis=1), work[:, slots:]], axis=1)
    keep = (row_tiles[:, None] >= col_tiles[None, :])[:, :, None, None]
    factored = jnp.where(keep, work, 0.0).transpose(0, 2, 1, 3)
    return (factored.reshape(matrix.shape), new_totals.reshape(checksum.shape))


def solution(mesh):
    return jax.shard_map(
        shards,
        mesh=mesh,
        in_specs=(
            P("row", None, None, "col", None, None),
            P("row", None, None, None, None),
            P("col"),
        ),
        out_specs=(P("row", None, None, "col", None, None), P("row", None, None, None, None)),
        check_vma=False,
    )
```

profile of v0, /device:TPU:0, one launch (start us, length us, event | category | flops | bytes accessed | tf_op | source)
XLA Modules:
  0.0 600.1 jit_solution(15367717784824096456)
XLA Ops:
  7.2 12.1 %copy.79 = f32[1,3,256,1,6,256]{2,5,4,1,3,0:T(8,128)} copy(f32[1,3,256,1,6,256]{5,3,4,2,1,0:T(1,128)} %param.6) | data formatting | bytes 9437184 | tf_op args[0]
  23.7 9.9 %all-reduce.2 = s32[4]{0:T(128)S(1)} all-reduce(s32[4]{0:T(128)S(1)} %dynamic-update-slice.10), channel_id=1, replica_groups=mesh['row'=8,'col'=4] {'col'}, use_global_device_ids=true, to_apply=%add.2 | all-reduce | flops 4 | bytes 32
  33.8 6.1 %copy.78 = f32[1,3,256,6,256]{2,4,3,1,0:T(8,128)} copy(f32[1,3,256,6,256]{4,2,3,1,0:T(8,128)} %param.7) | data formatting | bytes 9437184 | tf_op args[1]
  39.9 2.7 slice.200
  44.4 43.6 %all-gather.3.cloned.1.call-done = f32[12,1,256,256]{3,2,1,0:T(8,128)} async-done(((f32[3,1,256,256]{3,2,1,0:T(8,128)}), f32[12,1,256,256]{3,2,1,0:T(8,128)}) %all-gather.3.cloned.1.call-update) | async-done | bytes 3145744 | tf_op jit(solution)/shard_map/all_gather | solution.py:33
  88.0 3.3 fusion.84
  91.3 2.3 copy.118
  96.2 2.4 copy.119
  98.5 1.8 broadcast_select_fusion.2
  101.6 1.6 fusion.15
  103.3 1.6 pad_maximum_fusion.3
  106.4 2.3 slice_bitcast_fusion.3
  108.7 2.5 pad_maximum_fusion.1
  114.0 52.6 %all-reduce.7.cloned.1.call-done = f32[3,3,256,256]{2,3,1,0:T(8,128)} async-done(((f32[3,3,256,256]{2,3,1,0:T(8,128)}), f32[3,3,256,256]{2,3,1,0:T(8,128)}) %all-reduce.7.cloned.1.call-update) | async-done | bytes 2359312 | tf_op jit(solution)/shard_map/psum | solution.py:58
  166.7 4.6 broadcast_select_fusion
  173.6 11.7 %cholesky.172 = f32[128,128]{1,0:T(8,128)S(1)} custom-call(f32[128,128]{1,0:T(8,128)S(1)} %cholesky.270), custom_call_target="Cholesky" | custom-call | tf_op jit(solution)/shard_map/jit(cholesky)/cholesky | solution.py:94
  185.4 9.8 %custom-call.15 = f32[1,128,128]{1,2,0:T(8,128)S(1)} custom-call(f32[1,128,128]{2,1,0:T(8,128)S(1)} %get-tuple-element.105), custom_call_target="InvertDiagBlocksLowerTriangular" | custom-call | tf_op jit(solution)/shard_map/jit(cholesky)/cholesky | solution.py:94
  195.7 11.7 %cholesky.189 = f32[128,128]{1,0:T(8,128)S(1)} custom-call(f32[128,128]{1,0:T(8,128)S(1)} %convolution_subtract_fusion.15), custom_call_target="Cholesky" | custom-call | tf_op jit(solution)/shard_map/jit(cholesky)/cholesky | solution.py:94
  210.1 3.8 while.6
  214.0 20.1 %custom-call.16 = f32[2,128,128]{1,2,0:T(8,128)S(1)} custom-call(f32[2,128,128]{2,1,0:T(8,128)S(1)} %get-tuple-element.28), custom_call_target="InvertDiagBlocksLowerTriangular" | custom-call | tf_op jit(solution)/shard_map/jit(_solve_triangular)/triangular_solve | solution.py:96
  235.0 1.6 fusion.20
  238.1 11.7 %cholesky.206 = f32[128,128]{1,0:T(8,128)S(1)} custom-call(f32[128,128]{1,0:T(8,128)S(1)} %cholesky.273), custom_call_target="Cholesky" | custom-call | tf_op jit(solution)/shard_map/jit(cholesky)/cholesky | solution.py:94
  249.9 9.8 %custom-call.17 = f32[1,128,128]{1,2,0:T(8,128)S(1)} custom-call(f32[1,128,128]{2,1,0:T(8,128)S(1)} %get-tuple-element.101), custom_call_target="InvertDiagBlocksLowerTriangular" | custom-call | tf_op jit(solution)/shard_map/jit(cholesky)/cholesky | solution.py:94
  260.2 11.7 %cholesky.223 = f32[128,128]{1,0:T(8,128)S(1)} custom-call(f32[128,128]{1,0:T(8,128)S(1)} %convolution_subtract_fusion.14), custom_call_target="Cholesky" | custom-call | tf_op jit(solution)/shard_map/jit(cholesky)/cholesky | solution.py:94
  275.4 4.2 while.7
  279.6 19.9 %custom-call.18 = f32[2,128,128]{1,2,0:T(8,128)S(1)} custom-call(f32[2,128,128]{2,1,0:T(8,128)S(1)} %get-tuple-element.29), custom_call_target="InvertDiagBlocksLowerTriangular" | custom-call | tf_op jit(solution)/shard_map/jit(_solve_triangular)/triangular_solve | solution.py:96
  302.6 2.2 convolution_subtract_fusion.8
  304.8 20.6 %all-reduce.9.cloned.1.call-done = f32[16,256,256]{1,2,0:T(8,128)} async-done(((f32[16,256,256]{1,2,0:T(8,128)}), f32[16,256,256]{1,2,0:T(8,128)}) %all-reduce.9.cloned.1.call-update) | async-done | bytes 4194320 | tf_op jit(solution)/shard_map/psum | solution.py:66
  326.8 2.5 slice_bitcast_fusion.1
  329.4 3.6 fusion.4
  333.2 2.4 copy-done.12
  336.6 4.7 maximum_bitcast_fusion
  345.1 11.7 %cholesky.240 = f32[128,128]{1,0:T(8,128)S(1)} custom-call(f32[128,128]{1,0:T(8,128)S(1)} %cholesky.276), custom_call_target="Cholesky" | custom-call | tf_op jit(solution)/shard_map/jit(cholesky)/cholesky | solution.py:94
  356.9 10.2 %custom-call.19 = f32[1,128,128]{1,2,0:T(8,128)S(1)} custom-call(f32[1,128,128]{2,1,0:T(8,128)S(1)} %get-tuple-element.97), custom_call_target="InvertDiagBlocksLowerTriangular" | custom-call | tf_op jit(solution)/shard_map/jit(cholesky)/cholesky | solution.py:94
  367.5 11.7 %cholesky.257 = f32[128,128]{1,0:T(8,128)S(1)} custom-call(f32[128,128]{1,0:T(8,128)S(1)} %convolution_subtract_fusion.13), custom_call_target="Cholesky" | custom-call | tf_op jit(solution)/shard_map/jit(cholesky)/cholesky | solution.py:94
  382.7 4.0 while.8
  386.6 20.3 %custom-call.20 = f32[2,128,128]{1,2,0:T(8,128)} custom-call(f32[2,128,128]{2,1,0:T(8,128)S(1)} %get-tuple-element.30), custom_call_target="InvertDiagBlocksLowerTriangular" | custom-call | tf_op jit(solution)/shard_map/jit(_solve_triangular)/triangular_solve | solution.py:96
  408.3 2.3 copy.98
  410.6 1.9 convolution_subtract_fusion.4
  412.6 2.0 bitcast_select_fusion.1
  414.6 2.5 copy.102
  417.0 1.8 copy.92
  424.1 1.7 bitcast_select_fusion
  427.0 51.3 %all-reduce.11.cloned.1.call-done = f32[3,256,12,256]{1,3,2,0:T(8,128)} async-done(((f32[3,256,12,256]{1,3,2,0:T(8,128)}), f32[3,256,12,256]{1,3,2,0:T(8,128)}) %all-reduce.11.cloned.1.call-update) | async-done | bytes 9437200 | tf_op jit(solution)/shard_map/psum | solution.py:84
  478.3 7.5 %fusion.83 = (f32[1,256,12,256]{1,3,2,0:T(8,128)}, f32[1,256,12,256]{1,3,2,0:T(8,128)S(1)}, f32[1,256,12,256]{1,3,2,0:T(8,128)}) fusion(f32[3,256,12,256]{1,3,2,0:T(8,128)} %all-reduce.11.cloned.1.call-done), kind=kLoop, calls=%fused_computation.179 | loop fusion | bytes 18874368 | tf_op jit(solution)/shard_map/slice | solution.py:112
  485.8 2.3 copy.105
  488.1 4.8 fusion.37
  492.9 3.7 copy.104
  496.6 5.2 convolution_subtract_fusion.1
  501.8 3.0 convolution_subtract_fusion.2
  504.9 3.0 fusion.34
  507.9 3.0 convolution_subtract_fusion
  510.9 4.7 fusion.32
  515.6 7.7 %pad_maximum_fusion = f32[768,3072]{1,0:T(8,128)} fusion(f32[256,3072]{1,0:T(8,128)} %fusion.32, f32[256,3072]{1,0:T(8,128)} %copy-done, f32[256,3072]{1,0:T(8,128)S(1)} %fusion.37), kind=kLoop, calls=%fused_computation.7 | loop fusion | flops 4718592 | bytes 18874368 | tf_op jit(solution)/shard_map/concatenate | solution.py:117
  523.3 10.0 %fusion.2 = f32[768,1536]{1,0:T(8,128)} fusion(f32[768,3072]{1,0:T(8,128)} %pad_maximum_fusion, f32[768,256]{1,0:T(8,128)} %get-tuple-element.114, f32[768,256]{1,0:T(8,128)} %get-tuple-element.112, f32[768,256]{1,0:T(8,128)} %bitcast.226), kind=kOutput, calls=%fused_computation.11 | convolution fusion | flops 5436997632 | bytes 11796480 | tf_op jit(solution)/shard_map/dot_general | solution.py:16
  533.3 7.7 %fusion = f32[768,1536]{1,0:T(8,128)} fusion(f32[768,3072]{1,0:T(8,128)S(1)} %copy-done.5, f32[768,256]{1,0:T(8,128)S(1)} %copy-done.39, f32[768,256]{1,0:T(8,128)S(1)} %copy-done.24, f32[768,256]{1,0:T(8,128)S(1)} %bitcast.227), kind=kOutput, calls=%fused_computation.9 | convolution fusion | flops 5436997632 | bytes 11796480 | tf_op jit(solution)/shard_map/dot_general | solution.py:16
  541.0 6.9 %reshape.317 = f32[3,256,6,256]{3,2,1,0:T(8,128)} reshape(f32[768,1536]{1,0:T(8,128)} %fusion.2) | data formatting | bytes 9437184 | tf_op jit(solution)/shard_map/reshape | solution.py:120
  547.9 6.0 %copy.106 = f32[3,256,6,256]{1,3,2,0:T(8,128)} copy(f32[3,256,6,256]{3,2,1,0:T(8,128)} %reshape.317) | data formatting | bytes 9437184 | tf_op jit(solution)/shard_map/reshape | solution.py:120
  553.9 4.4 bitcast_subtract_fusion
  560.6 2.7 fusion.5
  563.3 12.1 %copy.109 = f32[1,3,256,1,6,256]{5,3,4,2,1,0:T(1,128)} copy(f32[1,3,256,1,6,256]{2,5,4,1,3,0:T(8,128)} %fusion.5) | data formatting | bytes 9437184
  575.4 7.1 %reshape.319 = f32[1,3,256,6,256]{4,3,2,1,0:T(8,128)} reshape(f32[768,1536]{1,0:T(8,128)} %fusion) | data formatting | bytes 9437184 | tf_op jit(solution)/shard_map/reshape | solution.py:121
  582.5 7.2 %copy_subtract_fusion = f32[1,3,256,6,256]{4,3,2,1,0:T(8,128)S(1)} fusion(f32[1,3,256,6,256]{4,3,2,1,0:T(8,128)} %reshape.319, f32[1,3,256,6,256]{4,2,3,1,0:T(8,128)} %param.7), kind=kLoop, calls=%fused_computation.8 | loop fusion | flops 1179648 | bytes 14155776 | tf_op jit(solution)/shard_map/sub | solution.py:122
  589.7 3.6 copy.110
  (235 shorter events, 57.1 us)
Async XLA Ops:
  7.2 80.9 %all-gather.3.cloned.1.call-start = ((), (), s32[]{:S(2)}) async-start(), calls=%async_computation.3 | async-start | bytes 3932160 | tf_op jit(solution)/shard_map/all_gather | solution.py:33
  19.3 3.1 copy-start.54
  21.7 145.0 %all-reduce.7.cloned.1.call-start = ((), (), s32[]{:S(2)}) async-start(), calls=%async_computation | async-start | bytes 4718592 | tf_op jit(solution)/shard_map/psum | solution.py:58
  42.7 0.6 copy-start.40
  42.7 1.7 copy-start.42
  43.4 0.9 copy-start.44
  43.4 0.9 copy-start.46
  88.0 5.6 copy-start.3
  96.2 4.2 copy-start.21
  98.5 3.0 copy-start.49
  104.9 220.5 %all-reduce.9.cloned.1.call-start = ((), (), s32[]{:S(2)}) async-start(), calls=%async_computation.1 | async-start | bytes 8388608 | tf_op jit(solution)/shard_map/psum | solution.py:66
  105.0 194.8 %copy-start.13 = (f32[256,256]{1,0:T(8,128)}, f32[256,256]{1,0:T(8,128)S(1)}, u32[]{:S(2)}) copy-start(f32[256,256]{1,0:T(8,128)S(1)} %fusion.31) | copy-start | bytes 786436
  171.3 307.1 %all-reduce.11.cloned.1.call-start = ((), (), s32[]{:S(2)}) async-start(), calls=%async_computation.2 | async-start | bytes 18874368 | tf_op jit(solution)/shard_map/psum | solution.py:84
  235.0 172.1 %copy-start.18 = (f32[128,256]{1,0:T(8,128)}, f32[128,256]{1,0:T(8,128)S(1)}, u32[]{:S(2)}) copy-start(f32[128,256]{1,0:T(8,128)S(1)} %fusion.53) | copy-start | bytes 393220
  279.6 45.7 %copy-start.52 = (s32[2,2]{1,0:T(2,128)}, s32[2,2]{1,0:T(2,128)S(1)}, u32[]{:S(2)}) copy-start(s32[2,2]{1,0:T(2,128)S(1)} %get-tuple-element.277) | copy-start | bytes 52
  299.8 41.5 %copy-start.15 = (f32[128,256]{1,0:T(8,128)}, f32[128,256]{1,0:T(8,128)S(1)}, u32[]{:S(2)}) copy-start(f32[128,256]{1,0:T(8,128)S(1)} %fusion.40) | copy-start | bytes 393220
  302.6 119.8 %copy-start.4 = (f32[256,256]{1,0:T(8,128)}, f32[256,256]{1,0:T(8,128)S(1)}, u32[]{:S(2)}) copy-start(f32[256,256]{1,0:T(8,128)S(1)} %fusion.22) | copy-start | bytes 786436
  325.4 4.0 slice-start
  326.8 2.5 slice-start.1
  333.0 3.7 copy-start.1
  333.0 2.6 copy-start.12
  341.3 0.9 copy-start.29
  341.3 1.0 copy-start.37
  342.4 40.3 %copy-start.53 = (s32[2,2]{1,0:T(2,128)S(1)}, s32[2,2]{1,0:T(2,128)}, u32[]{:S(2)}) copy-start(s32[2,2]{1,0:T(2,128)} %copy-done.52) | copy-start | bytes 52
  343.0 80.3 %copy-start.10 = (f32[256,256]{1,0:T(8,128)}, f32[256,256]{1,0:T(8,128)S(1)}, u32[]{:S(2)}) copy-start(f32[256,256]{1,0:T(8,128)S(1)} %fusion.36) | copy-start | bytes 786436
  343.0 64.0 %copy-start.38 = (f32[256,256]{1,0:T(8,128)S(1)}, f32[256,256]{1,0:T(8,128)}, u32[]{:S(2)}) copy-start(f32[256,256]{1,0:T(8,128)} %get-tuple-element.68) | copy-start | bytes 786436
  344.5 62.6 %copy-start.50 = (pred[3]{0:T(512)(128)(4,1)S(1)}, pred[3]{0:T(512)(128)(4,1)}, u32[]{:S(2)}) copy-start(pred[3]{0:T(512)(128)(4,1)} %get-tuple-element.116) | copy-start | bytes 13
  344.5 62.6 %copy-start.51 = (pred[3]{0:T(512)(128)(4,1)S(1)}, pred[3]{0:T(512)(128)(4,1)}, u32[]{:S(2)}) copy-start(pred[3]{0:T(512)(128)(4,1)} %get-tuple-element.117) | copy-start | bytes 13
  386.6 20.4 %copy-start.32 = (f32[256,256]{1,0:T(8,128)}, f32[256,256]{1,0:T(8,128)S(1)}, u32[]{:S(2)}) copy-start(f32[256,256]{1,0:T(8,128)S(1)} %get-tuple-element.272) | copy-start | bytes 786436
  408.0 6.6 %copy-start.6 = (f32[3,256,256]{1,2,0:T(8,128)}, f32[3,256,256]{1,2,0:T(8,128)S(1)}, u32[]{:S(2)}) copy-start(f32[3,256,256]{1,2,0:T(8,128)S(1)} %fusion.9) | copy-start | bytes 2359300
  408.0 4.6 copy-start.16
  408.0 4.6 copy-start.25
  408.0 4.6 copy-start.30
  408.3 14.1 %copy-start.8 = (f32[3,256,256]{2,1,0:T(8,128)}, f32[3,256,256]{2,1,0:T(8,128)S(1)}, u32[]{:S(2)}) copy-start(f32[3,256,256]{2,1,0:T(8,128)S(1)} %copy.97) | copy-start | bytes 2359300
  412.6 6.3 %copy-start.14 = (f32[256,256]{1,0:T(8,128)S(1)}, f32[256,256]{1,0:T(8,128)}, u32[]{:S(2)}) copy-start(f32[256,256]{1,0:T(8,128)} %copy-done.13) | copy-start | bytes 786436
  414.6 7.8 %copy-start.22 = (f32[3,1,256,256]{3,2,0,1:T(8,128)S(1)}, f32[3,1,256,256]{3,2,0,1:T(8,128)}, u32[]{:S(2)}) copy-start(f32[3,1,256,256]{3,2,0,1:T(8,128)} %copy.93) | copy-start | bytes 2359300
  414.6 8.7 %copy-start.23 = (f32[768,256]{1,0:T(8,128)S(1)}, f32[768,256]{1,0:T(8,128)}, u32[]{:S(2)}) copy-start(f32[768,256]{1,0:T(8,128)} %get-tuple-element.112) | copy-start | bytes 2359300
  418.9 5.2 copy-start.26
  420.1 5.7 copy-start.27
  422.4 3.4 copy-start.33
  496.6 5.2 copy-start.2
  501.8 3.0 copy-start.17
  501.8 3.0 copy-start.31
  504.8 3.0 copy-start.11
  507.8 3.1 copy-start
  507.8 3.1 copy-start.28
  507.8 3.1 copy-start.34
  523.3 10.0 %copy-start.5 = (f32[768,3072]{1,0:T(8,128)S(1)}, f32[768,3072]{1,0:T(8,128)}, u32[]{:S(2)}) copy-start(f32[768,3072]{1,0:T(8,128)} %pad_maximum_fusion) | copy-start | bytes 28311556
  523.3 10.0 %copy-start.9 = (f32[3,256,256]{2,1,0:T(8,128)S(1)}, f32[3,256,256]{2,1,0:T(8,128)}, u32[]{:S(2)}) copy-start(f32[3,256,256]{2,1,0:T(8,128)} %copy-done.8) | copy-start | bytes 2359300
  523.3 10.0 %copy-start.24 = (f32[768,256]{1,0:T(8,128)S(1)}, f32[768,256]{1,0:T(8,128)}, u32[]{:S(2)}) copy-start(f32[768,256]{1,0:T(8,128)} %get-tuple-element.112) | copy-start | bytes 2359300
  523.3 10.0 %copy-start.39 = (f32[768,256]{1,0:T(8,128)S(1)}, f32[768,256]{1,0:T(8,128)}, u32[]{:S(2)}) copy-start(f32[768,256]{1,0:T(8,128)} %get-tuple-element.114) | copy-start | bytes 2359300
  558.3 1.1 copy-start.7
  558.3 1.4 copy-start.19
  558.3 1.6 copy-start.20
  558.3 1.6 copy-start.35
  558.3 1.7 copy-start.36
  558.3 1.7 copy-start.41
  558.3 1.7 copy-start.43
  558.4 1.7 copy-start.45
  558.4 1.7 copy-start.47
  560.0 0.6 copy-start.48
Sparse Core Ops, SparseCore 0:
  21.8 66.1 all-gather.2
  105.0 61.5 all-reduce.6
  171.4 153.9 all-reduce.8
  341.5 136.7 all-reduce.10
where the time goes:
time: 606 us; the launch traced here: 600 us
  other arithmetic  213 us (35%)
  waiting for transfers between devices  168 us (28%)
  local copies, waits for them, and re-layouts  122 us (20%)
  matrix products  65.9 us (11%)
  between operations  19.8 us (3%)
  blocking collectives  9.92 us (2%)
    another operation x20, other arithmetic, shards(): factor[k, k] = jnp.linalg.cholesky(tile)  104 us
    another operation x7, other arithmetic, shards(): jax.scipy.linalg.solve_triangular(factor[k, k], identity, lower=True)  62.5 us
    psum x1, waiting for transfers between devices, shards(): lead = lax.psum(lead, 'row')  52.6 us
    psum x1, waiting for transfers between devices, shards(): tops = lax.psum(tops, 'row')  51.3 us
    unnamed x124, local copies, waits for them, and re-layouts  46.6 us
    all_gather x1, waiting for transfers between devices, shards(): gathered = lax.all_gather(own[:, :slots], 'col', axis=0)  43.6 us
    dot_general x8, matrix products, dot(): return lax.dot_general(a, b, (((1,), (0,)), ((), ())), precision=precision)  41.3 us
    psum x1, waiting for transfers between devices, shards(): summed = lax.psum(jnp.where(lost, 0.0, packed), 'col')  20.6 us
  transfers between devices with their start and end apart: 4, of which 4 were waited for; matrix products, arithmetic and copies ran while one was open for 39% of the time, Pallas kernels for 0%

commit v1 on v0

--- a/solution.py
+++ b/solution.py
@@ -81,7 +81,9 @@
             for i in range(PANELS)
         ]
     )
-    tops = lax.psum(tops, "row")
+    tops = tops
+    for hop in (1, 2, 4):
+        tops = tops + lax.ppermute(tops, "row", [(dev, dev ^ hop) for dev in range(8)])
     identity = jnp.eye(width, dtype=jnp.float32)
     factor = {}
     inverse = []

time: 606 us -> 936 us (1.54)
  waiting for transfers between devices: 168 us -> 440 us
  other arithmetic: 213 us -> 246 us
  local copies, waits for them, and re-layouts: 122 us -> 134 us
    ppermute x0 -> x3, waiting for transfers between devices: none -> 185 us  [shards(): lax.ppermute(tops, 'row', [(dev, dev ^ hop) for dev in range(8)])]
    psum x1, waiting for transfers between devices: 20.6 us -> 151 us  [shards(): summed = lax.psum(jnp.where(lost, 0.0, packed), 'col')]
    psum x1 -> x0, waiting for transfers between devices: 51.3 us -> none  [shards(): tops = lax.psum(tops, 'row')]
    add x0 -> x2, other arithmetic: none -> 18.7 us  [shards(): tops + lax.ppermute(tops, 'row', [(dev, dev ^ hop) for dev in range(8)])]
    unnamed x124 -> x134, local copies, waits for them, and re-layouts: 46.6 us -> 48.8 us
  transfers between devices with their start and end apart: 4 -> 6, of which waited for: 4 -> 6; matrix products, arithmetic and copies ran while one was open for 39% -> 27% of each run, Pallas kernels for 0% -> 0%
where the time goes in v1:
time: 936 us; the launch traced here: 927 us
  waiting for transfers between devices  440 us (47%)
  other arithmetic  246 us (26%)
  local copies, waits for them, and re-layouts  134 us (14%)
  matrix products  74.6 us (8%)
  between operations  19.7 us (2%)
  blocking collectives  9.92 us (1%)
    ppermute x3, waiting for transfers between devices, shards(): lax.ppermute(tops, 'row', [(dev, dev ^ hop) for dev in range(8)])  185 us
    psum x1, waiting for transfers between devices, shards(): summed = lax.psum(jnp.where(lost, 0.0, packed), 'col')  151 us
    another operation x20, other arithmetic, shards(): factor[k, k] = jnp.linalg.cholesky(tile)  105 us
    another operation x7, other arithmetic, shards(): jax.scipy.linalg.solve_triangular(factor[k, k], identity, lower=True)  63.3 us
    psum x1, waiting for transfers between devices, shards(): lead = lax.psum(lead, 'row')  55.7 us
    unnamed x134, local copies, waits for them, and re-layouts  48.8 us
    all_gather x1, waiting for transfers between devices, shards(): gathered = lax.all_gather(own[:, :slots], 'col', axis=0)  48 us
    dot_general x8, matrix products, dot(): return lax.dot_general(a, b, (((1,), (0,)), ((), ())), precision=precision)  47.2 us
  transfers between devices with their start and end apart: 6, of which 6 were waited for; matrix products, arithmetic and copies ran while one was open for 27% of the time, Pallas kernels for 0%

profile of v1, /device:TPU:0, one launch (start us, length us, event | category | flops | bytes accessed | tf_op | source)
XLA Modules:
  0.0 927.5 jit_solution(17561200092217458623)
XLA Ops:
  7.2 12.1 %copy.79 = f32[1,3,256,1,6,256]{2,5,4,1,3,0:T(8,128)} copy(f32[1,3,256,1,6,256]{5,3,4,2,1,0:T(1,128)} %param.6) | data formatting | bytes 9437184 | tf_op args[0]
  23.7 9.9 %all-reduce.2 = s32[4]{0:T(128)S(1)} all-reduce(s32[4]{0:T(128)S(1)} %dynamic-update-slice.10), channel_id=1, replica_groups=mesh['row'=8,'col'=4] {'col'}, use_global_device_ids=true, to_apply=%add.2 | all-reduce | flops 4 | bytes 32
  33.8 6.1 copy.78
  40.0 48.0 %all-gather.3.cloned.1.call-done = f32[12,1,256,256]{3,2,1,0:T(8,128)} async-done(((f32[3,1,256,256]{3,2,1,0:T(8,128)}), f32[12,1,256,256]{3,2,1,0:T(8,128)}) %all-gather.3.cloned.1.call-update) | async-done | bytes 3145744 | tf_op jit(solution)/shard_map/all_gather | solution.py:33
  88.0 3.2 fusion.88
  91.2 2.3 copy.118
  96.2 2.4 copy.119
  106.8 2.3 slice_bitcast_fusion.3
  109.1 2.4 pad_maximum_fusion.2
  111.5 55.7 %all-reduce.6.cloned.1.call-done = f32[3,3,256,256]{2,3,1,0:T(8,128)} async-done(((f32[3,3,256,256]{2,3,1,0:T(8,128)}), f32[3,3,256,256]{2,3,1,0:T(8,128)}) %all-reduce.6.cloned.1.call-update) | async-done | bytes 2359312 | tf_op jit(solution)/shard_map/psum | solution.py:58
  167.2 4.6 broadcast_select_fusion
  171.8 2.8 slice.200
  174.5 150.8 %all-reduce.8.cloned.1.call-done = f32[16,256,256]{1,2,0:T(8,128)} async-done(((f32[16,256,256]{1,2,0:T(8,128)}), f32[16,256,256]{1,2,0:T(8,128)}) %all-reduce.8.cloned.1.call-update) | async-done | bytes 4194320 | tf_op jit(solution)/shard_map/psum | solution.py:66
  326.8 2.5 slice_bitcast_fusion.1
  329.4 3.7 fusion.4
  333.1 2.2 copy-done.4
  337.6 5.0 pad_maximum_fusion
  342.6 14.9 %collective-permute-done = f32[3,12,256,256]{2,3,1,0:T(8,128)S(1)} collective-permute-done((f32[3,12,256,256]{2,3,1,0:T(8,128)}, f32[3,12,256,256]{2,3,1,0:T(8,128)S(1)}, u32[]{:S(2)}, u32[]{:S(2)}) %collective-permute-start) | collective-permute-done | bytes 9437216 | tf_op jit(solution)/shard_map/ppermute | solution.py:86
  357.5 5.8 fusion.81
  368.1 2.3 copy.93
  370.4 2.3 copy.100
  378.0 11.7 %cholesky.172 = f32[128,128]{1,0:T(8,128)S(1)} custom-call(f32[128,128]{1,0:T(8,128)S(1)} %cholesky.270), custom_call_target="Cholesky" | custom-call | tf_op jit(solution)/shard_map/jit(cholesky)/cholesky | solution.py:96
  390.9 9.8 %custom-call.15 = f32[1,128,128]{1,2,0:T(8,128)S(1)} custom-call(f32[1,128,128]{2,1,0:T(8,128)S(1)} %get-tuple-element.105), custom_call_target="InvertDiagBlocksLowerTriangular" | custom-call | tf_op jit(solution)/shard_map/jit(cholesky)/cholesky | solution.py:96
  403.5 11.7 %cholesky.189 = f32[128,128]{1,0:T(8,128)S(1)} custom-call(f32[128,128]{1,0:T(8,128)S(1)} %convolution_subtract_fusion.12), custom_call_target="Cholesky" | custom-call | tf_op jit(solution)/shard_map/jit(cholesky)/cholesky | solution.py:96
  420.3 148.9 %collective-permute-done.1 = f32[3,12,256,256]{2,3,1,0:T(8,128)} collective-permute-done((f32[3,12,256,256]{2,3,1,0:T(8,128)}, f32[3,12,256,256]{2,3,1,0:T(8,128)}, u32[]{:S(2)}, u32[]{:S(2)}) %collective-permute-start.1) | collective-permute-done | bytes 9437216 | tf_op jit(solution)/shard_map/ppermute | solution.py:86
  569.2 12.9 %fusion.128 = f32[3,12,256,256]{2,3,1,0:T(8,128)} fusion(f32[3,12,256,256]{2,3,1,0:T(8,128)} %collective-permute-done.1, f32[3,12,256,256]{2,3,1,0:T(8,128)} %copy-done.2, f32[1,12,256,256]{2,3,1,0:T(8,128)} %copy-done.1, f32[1,12,256,256]{2,3,1,0:T(8,128)} %copy-done, f32[1,12,256,256]{2,3,1,0:T(8,128)S(1)} %get-tuple-element.86), kind=kLoop, calls=%fused_computation.186 | loop fusion | flops 9437184 | bytes 37748736 | tf_op jit(solution)/shard_map/add | solution.py:86
  583.6 5.9 while.6
  584.2 2.3 bitcast_dynamic-update-slice_fusion.6
  587.2 2.3 bitcast_dynamic-update-slice_fusion.6
  589.4 20.1 %custom-call.16 = f32[2,128,128]{1,2,0:T(8,128)S(1)} custom-call(f32[2,128,128]{2,1,0:T(8,128)S(1)} %get-tuple-element.28), custom_call_target="InvertDiagBlocksLowerTriangular" | custom-call | tf_op jit(solution)/shard_map/jit(_solve_triangular)/triangular_solve | solution.py:98
  614.5 11.7 %cholesky.206 = f32[128,128]{1,0:T(8,128)S(1)} custom-call(f32[128,128]{1,0:T(8,128)S(1)} %cholesky.273), custom_call_target="Cholesky" | custom-call | tf_op jit(solution)/shard_map/jit(cholesky)/cholesky | solution.py:96
  626.2 9.8 %custom-call.17 = f32[1,128,128]{1,2,0:T(8,128)S(1)} custom-call(f32[1,128,128]{2,1,0:T(8,128)S(1)} %get-tuple-element.101), custom_call_target="InvertDiagBlocksLowerTriangular" | custom-call | tf_op jit(solution)/shard_map/jit(cholesky)/cholesky | solution.py:96
  636.5 11.7 %cholesky.223 = f32[128,128]{1,0:T(8,128)S(1)} custom-call(f32[128,128]{1,0:T(8,128)S(1)} %convolution_subtract_fusion.11), custom_call_target="Cholesky" | custom-call | tf_op jit(solution)/shard_map/jit(cholesky)/cholesky | solution.py:96
  650.9 4.0 while.7
  654.9 19.9 %custom-call.18 = f32[2,128,128]{1,2,0:T(8,128)S(1)} custom-call(f32[2,128,128]{2,1,0:T(8,128)S(1)} %get-tuple-element.29), custom_call_target="InvertDiagBlocksLowerTriangular" | custom-call | tf_op jit(solution)/shard_map/jit(_solve_triangular)/triangular_solve | solution.py:98
  681.5 11.7 %cholesky.240 = f32[128,128]{1,0:T(8,128)S(1)} custom-call(f32[128,128]{1,0:T(8,128)S(1)} %cholesky.276), custom_call_target="Cholesky" | custom-call | tf_op jit(solution)/shard_map/jit(cholesky)/cholesky | solution.py:96
  693.3 9.8 %custom-call.19 = f32[1,128,128]{1,2,0:T(8,128)S(1)} custom-call(f32[1,128,128]{2,1,0:T(8,128)S(1)} %get-tuple-element.97), custom_call_target="InvertDiagBlocksLowerTriangular" | custom-call | tf_op jit(solution)/shard_map/jit(cholesky)/cholesky | solution.py:96
  703.6 12.1 %cholesky.257 = f32[128,128]{1,0:T(8,128)S(1)} custom-call(f32[128,128]{1,0:T(8,128)S(1)} %convolution_subtract_fusion.10), custom_call_target="Cholesky" | custom-call | tf_op jit(solution)/shard_map/jit(cholesky)/cholesky | solution.py:96
  719.0 5.2 while.8
  724.2 20.3 %custom-call.20 = f32[2,128,128]{1,2,0:T(8,128)} custom-call(f32[2,128,128]{2,1,0:T(8,128)S(1)} %get-tuple-element.30), custom_call_target="InvertDiagBlocksLowerTriangular" | custom-call | tf_op jit(solution)/shard_map/jit(_solve_triangular)/triangular_solve | solution.py:98
  750.5 2.0 bitcast_select_fusion.1
  752.5 2.4 copy.102
  764.8 21.6 %collective-permute-done.2 = f32[3,12,256,256]{2,3,1,0:T(8,128)} collective-permute-done((f32[3,12,256,256]{2,3,1,0:T(8,128)}, f32[3,12,256,256]{2,3,1,0:T(8,128)}, u32[]{:S(2)}, u32[]{:S(2)}) %collective-permute-start.2) | collective-permute-done | bytes 9437216 | tf_op jit(solution)/shard_map/ppermute | solution.py:86
  786.4 11.7 %add_bitcast_fusion = f32[3,256,12,256]{1,3,2,0:T(8,128)} fusion(f32[3,12,256,256]{2,3,1,0:T(8,128)} %fusion.128, f32[3,12,256,256]{2,3,1,0:T(8,128)} %collective-permute-done.2), kind=kLoop, calls=%fused_computation.8 | loop fusion | flops 2359296 | bytes 28311552 | tf_op jit(solution)/shard_map/transpose | solution.py:111
  798.1 7.6 fusion.87
  805.8 2.8 fusion.40
  808.6 4.7 fusion.89
  813.3 4.4 fusion.90
  817.7 3.6 copy.104
  821.4 4.9 fusion.9
  826.3 4.5 fusion.91
  830.8 3.8 copy.105
  834.7 8.3 fusion.6
  842.9 7.7 pad_maximum_fusion.1
  850.6 10.0 %fusion.2 = f32[768,1536]{1,0:T(8,128)} fusion(f32[768,3072]{1,0:T(8,128)} %pad_maximum_fusion.1, f32[768,256]{1,0:T(8,128)} %get-tuple-element.114, f32[768,256]{1,0:T(8,128)} %get-tuple-element.112, f32[768,256]{1,0:T(8,128)} %bitcast.224), kind=kOutput, calls=%fused_computation.12 | convolution fusion | flops 5436997632 | bytes 11796480 | tf_op jit(solution)/shard_map/dot_general | solution.py:16
  860.6 7.6 fusion
  868.2 6.9 reshape.317
  875.2 6.2 copy.106
  881.4 4.4 bitcast_subtract_fusion
  888.2 2.7 fusion.5
  890.9 12.1 %copy.109 = f32[1,3,256,1,6,256]{5,3,4,2,1,0:T(1,128)} copy(f32[1,3,256,1,6,256]{2,5,4,1,3,0:T(8,128)} %fusion.5) | data formatting | bytes 9437184
  903.0 6.9 reshape.319
  909.9 7.2 copy_subtract_fusion
  917.1 3.6 copy.110
  (251 shorter events, 82.1 us)
Async XLA Ops:
  7.2 80.8 %all-gather.3.cloned.1.call-start = ((), (), s32[]{:S(2)}) async-start(), calls=%async_computation.2 | async-start | bytes 3932160 | tf_op jit(solution)/shard_map/all_gather | solution.py:33
  19.3 3.1 copy-start.59
  21.7 145.5 %all-reduce.6.cloned.1.call-start = ((), (), s32[]{:S(2)}) async-start(), calls=%async_computation | async-start | bytes 4718592 | tf_op jit(solution)/shard_map/psum | solution.py:58
  88.0 5.5 copy-start.5
  94.7 3.9 copy-start.29
  96.2 4.9 copy-start.28
  98.6 2.8 copy-start.56
  100.2 0.9 copy-start.16
  100.2 2.6 copy-start.17
  102.8 0.9 copy-start.18
  105.4 219.9 %all-reduce.8.cloned.1.call-start = ((), (), s32[]{:S(2)}) async-start(), calls=%async_computation.1 | async-start | bytes 8388608 | tf_op jit(solution)/shard_map/psum | solution.py:66
  325.3 4.0 slice-start
  326.8 2.5 slice-start.1
  333.1 2.2 copy-start.4
  335.3 1.4 copy-start.15
  337.5 19.9 %copy-start = (f32[1,12,256,256]{2,3,1,0:T(8,128)}, f32[1,12,256,256]{2,3,1,0:T(8,128)S(1)}, u32[]{:S(2)}) copy-start(f32[1,12,256,256]{2,3,1,0:T(8,128)S(1)} %get-tuple-element.87) | copy-start | bytes 9437188
  337.6 19.9 %copy-start.1 = (f32[1,12,256,256]{2,3,1,0:T(8,128)}, f32[1,12,256,256]{2,3,1,0:T(8,128)S(1)}, u32[]{:S(2)}) copy-start(f32[1,12,256,256]{2,3,1,0:T(8,128)S(1)} %get-tuple-element.88) | copy-start | bytes 9437188
  342.6 14.9 %collective-permute-start = (f32[3,12,256,256]{2,3,1,0:T(8,128)}, f32[3,12,256,256]{2,3,1,0:T(8,128)S(1)}, u32[]{:S(2)}, u32[]{:S(2)}) collective-permute-start(f32[3,12,256,256]{2,3,1,0:T(8,128)} %pad_maximum_fusion), channel_id=1, source_target_pairs={{0,4},{4,0},{8,12},{12,8},{16,20},{20,16},{24,28},{28,24},{1,5},{5... | collective-permute-start | bytes 28311560 | tf_op jit(solution)/shard_map/ppermute | solution.py:86
  357.5 6.4 copy-start.2
  363.9 205.3 %collective-permute-start.1 = (f32[3,12,256,256]{2,3,1,0:T(8,128)}, f32[3,12,256,256]{2,3,1,0:T(8,128)}, u32[]{:S(2)}, u32[]{:S(2)}) collective-permute-start(f32[3,12,256,256]{2,3,1,0:T(8,128)} %fusion.81), channel_id=1, source_target_pairs={{0,8},{4,12},{8,0},{12,4},{16,24},{20,28},{24,16},{28,20},{1,9},{5... | collective-permute-start | bytes 28311560 | tf_op jit(solution)/shard_map/ppermute | solution.py:86
  365.4 1.5 copy-start.49
  367.4 242.4 %copy-start.20 = (f32[256,256]{1,0:T(8,128)}, f32[256,256]{1,0:T(8,128)S(1)}, u32[]{:S(2)}) copy-start(f32[256,256]{1,0:T(8,128)S(1)} %fusion.36) | copy-start | bytes 786436
  377.2 0.7 copy-start.45
  420.3 163.2 %copy-start.58 = (s32[2]{0:T(128)S(1)}, s32[2]{0:T(128)}, u32[]{:S(2)}) copy-start(s32[2]{0:T(128)} %iota_multiply_fusion) | copy-start | bytes 28
  582.0 204.4 %collective-permute-start.2 = (f32[3,12,256,256]{2,3,1,0:T(8,128)}, f32[3,12,256,256]{2,3,1,0:T(8,128)}, u32[]{:S(2)}, u32[]{:S(2)}) collective-permute-start(f32[3,12,256,256]{2,3,1,0:T(8,128)} %fusion.128), channel_id=1, source_target_pairs={{0,16},{4,20},{8,24},{12,28},{16,0},{20,4},{24,8},{28,12},{1,17},{... | collective-permute-start | bytes 28311560 | tf_op jit(solution)/shard_map/ppermute | solution.py:86
  611.3 134.1 %copy-start.24 = (f32[128,256]{1,0:T(8,128)}, f32[128,256]{1,0:T(8,128)S(1)}, u32[]{:S(2)}) copy-start(f32[128,256]{1,0:T(8,128)S(1)} %fusion.56) | copy-start | bytes 393220
  611.3 63.5 %copy-start.21 = (f32[256,256]{1,0:T(8,128)S(1)}, f32[256,256]{1,0:T(8,128)}, u32[]{:S(2)}) copy-start(f32[256,256]{1,0:T(8,128)} %copy-done.20) | copy-start | bytes 786436
  654.9 23.9 %copy-start.57 = (s32[2,2]{1,0:T(2,128)}, s32[2,2]{1,0:T(2,128)S(1)}, u32[]{:S(2)}) copy-start(s32[2,2]{1,0:T(2,128)S(1)} %get-tuple-element.275) | copy-start | bytes 52
  675.1 75.4 %copy-start.22 = (f32[128,256]{1,0:T(8,128)}, f32[128,256]{1,0:T(8,128)S(1)}, u32[]{:S(2)}) copy-start(f32[128,256]{1,0:T(8,128)S(1)} %fusion.43) | copy-start | bytes 393220
  675.7 3.7 copy-start.36
  677.3 83.0 %copy-start.6 = (f32[256,256]{1,0:T(8,128)}, f32[256,256]{1,0:T(8,128)S(1)}, u32[]{:S(2)}) copy-start(f32[256,256]{1,0:T(8,128)S(1)} %fusion.27) | copy-start | bytes 786436
  679.4 81.7 %copy-start.13 = (f32[256,256]{1,0:T(8,128)}, f32[256,256]{1,0:T(8,128)S(1)}, u32[]{:S(2)}) copy-start(f32[256,256]{1,0:T(8,128)S(1)} %fusion.39) | copy-start | bytes 786436
  679.4 65.1 %copy-start.44 = (f32[256,256]{1,0:T(8,128)S(1)}, f32[256,256]{1,0:T(8,128)}, u32[]{:S(2)}) copy-start(f32[256,256]{1,0:T(8,128)} %get-tuple-element.68) | copy-start | bytes 786436
  680.9 64.5 %copy-start.19 = (f32[3,1,256,256]{2,3,1,0:T(8,128)S(1)}, f32[3,1,256,256]{2,3,1,0:T(8,128)}, u32[]{:S(2)}) copy-start(f32[3,1,256,256]{2,3,1,0:T(8,128)} %copy-done.18) | copy-start | bytes 2359300
  724.2 21.1 %copy-start.39 = (f32[256,256]{1,0:T(8,128)}, f32[256,256]{1,0:T(8,128)S(1)}, u32[]{:S(2)}) copy-start(f32[256,256]{1,0:T(8,128)S(1)} %get-tuple-element.270) | copy-start | bytes 786436
  745.4 5.1 copy-start.37
  747.2 5.3 copy-start.9
  747.5 12.8 %copy-start.11 = (f32[3,256,256]{2,1,0:T(8,128)}, f32[3,256,256]{2,1,0:T(8,128)S(1)}, u32[]{:S(2)}) copy-start(f32[3,256,256]{2,1,0:T(8,128)S(1)} %copy.97) | copy-start | bytes 2359300
  752.5 7.8 copy-start.30
  752.5 8.6 copy-start.31
  756.7 5.2 copy-start.33
  757.9 5.7 copy-start.34
  760.3 3.4 copy-start.40
  798.1 7.6 copy-start.25
  808.6 4.7 copy-start.7
  817.7 3.6 copy-start.23
  817.7 3.6 copy-start.38
  821.4 4.9 copy-start.14
  826.3 4.5 copy-start.3
  830.8 3.8 copy-start.35
  830.8 3.9 copy-start.41
  850.6 10.0 %copy-start.8 = (f32[768,3072]{1,0:T(8,128)S(1)}, f32[768,3072]{1,0:T(8,128)}, u32[]{:S(2)}) copy-start(f32[768,3072]{1,0:T(8,128)} %pad_maximum_fusion.1) | copy-start | bytes 28311556
  850.6 10.0 %copy-start.12 = (f32[3,256,256]{2,1,0:T(8,128)S(1)}, f32[3,256,256]{2,1,0:T(8,128)}, u32[]{:S(2)}) copy-start(f32[3,256,256]{2,1,0:T(8,128)} %copy-done.11) | copy-start | bytes 2359300
  850.6 10.0 %copy-start.32 = (f32[768,256]{1,0:T(8,128)S(1)}, f32[768,256]{1,0:T(8,128)}, u32[]{:S(2)}) copy-start(f32[768,256]{1,0:T(8,128)} %get-tuple-element.112) | copy-start | bytes 2359300
  850.6 10.0 %copy-start.46 = (f32[768,256]{1,0:T(8,128)S(1)}, f32[768,256]{1,0:T(8,128)}, u32[]{:S(2)}) copy-start(f32[768,256]{1,0:T(8,128)} %get-tuple-element.114) | copy-start | bytes 2359300
  885.8 1.1 copy-start.10
  885.8 1.4 copy-start.26
  885.8 1.6 copy-start.27
  885.8 1.6 copy-start.42
  885.8 1.7 copy-start.43
  885.8 1.7 copy-start.48
  885.9 1.7 copy-start.50
  885.9 1.7 copy-start.52
  885.9 1.7 copy-start.54
  (4 other events, 2.6 us)
Sparse Core Ops, SparseCore 0:
  21.8 66.1 all-gather.2
  105.5 61.6 all-reduce.5
  171.9 153.3 all-reduce.7
